TPU v7x, 32 devices: a whole 2x2x4 slice. The times are simulated.
32 devices in a mesh: dp: 4 (over x, core), context: 8 (over z, y).
Axes of the slice: x: 2, y: 2, z: 4, core: 2. Of those that a mesh axis runs over, the one named last changes fastest.
Arguments:
- signal: bfloat16 [8192, 2048], P('context', 'dp'), may hold values from -6 to 6
- gating: bfloat16 [8192, 2048], P('context', 'dp'), may hold values from -6 to 6
- writer: bfloat16 [8192, 128], P('context'), may hold values from -2 to 2
- reader: bfloat16 [8192, 128], P('context'), may hold values from -2 to 2
- step_raw: float32 [8192, 32], P('context', 'dp'), may hold values from -7 to -1
- decay_log: float32 [32], P('dp'), may hold values from -12 to 1
- skip_gain: float32 [32], P('dp'), may hold values from 0.5 to 2
- norm_gain: float32 [2048], P('dp'), may hold values from 0.25 to 1.75
- cotangent: bfloat16 [8192, 2048], P('context', 'dp'), may hold values from -6 to 6
Outputs:
- grad_signal: bfloat16 [8192, 2048], P('context', 'dp')
- grad_gating: bfloat16 [8192, 2048], P('context', 'dp')
- grad_bc: float32 [8192, 256], P('context', 'dp')
- grad_step: float32 [8192, 32], P('context', 'dp')
All inputs are finite; a program needn't handle non-finite values.
Results may differ from a plain program's by a relative error of at most 0.0011.
Values sent between devices are 32-bit elements; how exact they have to be, the bound alone decides.
No kernel may reach another device: no remote copies, remote signals or barrier semaphores. Data moves between devices by JAX's collectives and lax.ppermute only.
A program may use at most 64 MiB of HBM per device.

v0:
```python
from functools import partial
import jax
import jax.numpy as jnp
from jax import lax
from jax.sharding import PartitionSpec as P

HEADS = 32
HEAD_DIM = 64
SPAN = 256
highest = lax.Precision.HIGHEST
epsilon = 1e-05


def block_step(state, pieces, decay_rate, skip_gain):
    signal_block, writer_block, reader_block, raw_block = pieces
    step_size = jax.nn.softplus(raw_block)
    log_decay = step_size * decay_rate[None, :]
    running = jnp.cumsum(log_decay, axis=0)
    length = raw_block.shape[0]
    causal = jnp.arange(length)[:, None] >= jnp.arange(length)[None, :]
    log_gaps = running[:, None, :] - running[None, :, :]
    decays = jnp.exp(jnp.where(causal[:, :, None], log_gaps, -jnp.inf))
    scores = jnp.dot(
        reader_block, writer_block.T, precision=highest, preferred_element_type=jnp.float32
    )
    mixing = scores[:, :, None] * decays * step_size[None, :, :]
    within = jnp.einsum("tsh,shp->thp", mixing, signal_block, precision=highest)
    across = jnp.exp(running)[:, :, None] * jnp.einsum(
        "tn,hpn->thp", reader_block, state, precision=highest
    )
    result = within + across + skip_gain[None, :, None] * signal_block
    weights = jnp.exp(running[-1][None, :] - running) * step_size
    new_state = jnp.exp(running[-1])[:, None, None] * state + jnp.einsum(
        "sh,shp,sn->hpn", weights, signal_block, writer_block, precision=highest
    )
    return (new_state, result)


def recurrence(signal, writer, reader, step_raw, start_state, decay_rate, skip_gain):
    tokens, head_count = step_raw.shape
    blocks = tokens // SPAN
    pieces = (
        signal.reshape(blocks, SPAN, head_count, HEAD_DIM),
        writer.reshape(blocks, SPAN, -1),
        reader.reshape(blocks, SPAN, -1),
        step_raw.reshape(blocks, SPAN, head_count),
    )
    advance = jax.checkpoint(partial(block_step, decay_rate=decay_rate, skip_gain=skip_gain))
    end_state, outputs = lax.scan(advance, start_state, pieces)
    return (outputs.reshape(tokens, head_count * HEAD_DIM), end_state)


def on_device(signal, gating, writer, reader, step_raw, decay_log, skip_gain, norm_gain, cotangent):
    tokens, head_count = step_raw.shape
    decay_rate = -jnp.exp(decay_log)
    signal_f = signal.astype(jnp.float32)
    writer_f = writer.astype(jnp.float32)
    reader_f = reader.astype(jnp.float32)
    step_size = jax.nn.softplus(step_raw)
    running = jnp.cumsum(step_size * decay_rate[None, :], axis=0)
    totals = running[-1]
    weights = jnp.exp(totals[None, :] - running) * step_size
    local_end = jnp.einsum(
        "sh,shp,sn->hpn",
        weights,
        signal_f.reshape(tokens, head_count, HEAD_DIM),
        writer_f,
        precision=highest,
    )
    all_totals = lax.all_gather(totals[None, :], "context", axis=0, tiled=True)
    inclusive = jnp.cumsum(all_totals, axis=0)
    exclusive = inclusive - all_totals
    position = lax.axis_index("context")
    devices = all_totals.shape[0]
    mine = (jnp.arange(devices) == position).astype(jnp.float32)
    inclusive_mine = jnp.dot(mine, inclusive, precision=highest, preferred_element_type=jnp.float32)
    exclusive_mine = jnp.dot(mine, exclusive, precision=highest, preferred_element_type=jnp.float32)
    pieces = lax.all_gather(local_end[None], "context", axis=0, tiled=True)
    indices = jnp.arange(pieces.shape[0])
    select = (indices[:, None] == jnp.arange(devices)[None, :]).astype(jnp.float32)
    inclusive_from = jnp.dot(
        select, inclusive, precision=highest, preferred_element_type=jnp.float32
    )
    factors = jnp.where(
        (indices < position)[:, None],
        jnp.exp(jnp.minimum(exclusive_mine[None, :] - inclusive_from, 0.0)),
        0.0,
    )
    incoming = jnp.einsum("fh,fhpn->hpn", factors, pieces, precision=highest)

    def local_pass(signal_in, writer_in, reader_in, raw_in, state_in):
        return recurrence(signal_in, writer_in, reader_in, raw_in, state_in, decay_rate, skip_gain)

    primal_out, pullback = jax.vjp(local_pass, signal_f, writer_f, reader_f, step_raw, incoming)
    output = primal_out[0]
    gating_f = gating.astype(jnp.float32)
    cotangent_f = cotangent.astype(jnp.float32)
    sigmoid = jax.nn.sigmoid(gating_f)
    activation = gating_f * sigmoid
    gated_output = output * activation
    weighted = norm_gain[None, :] * cotangent_f
    statistics = lax.psum(
        (jnp.sum(gated_output * gated_output, axis=1), jnp.sum(weighted * gated_output, axis=1)),
        "dp",
    )
    full_width = HEADS * HEAD_DIM
    scaling = lax.rsqrt(statistics[0] / full_width + epsilon)
    grad_gated = (
        weighted * scaling[:, None]
        - gated_output * (scaling * scaling * scaling * statistics[1] / full_width)[:, None]
    )
    grad_output = grad_gated * activation
    grad_gating = grad_gated * output * sigmoid * (1.0 + gating_f * (1.0 - sigmoid))
    influence = jnp.einsum(
        "th,thp,tn->hpn",
        jnp.exp(running),
        grad_output.reshape(tokens, head_count, HEAD_DIM),
        reader_f,
        precision=highest,
    )
    pieces = lax.all_gather(influence[None], "context", axis=0, tiled=True)
    indices = jnp.arange(pieces.shape[0])
    select = (indices[:, None] == jnp.arange(devices)[None, :]).astype(jnp.float32)
    exclusive_from = jnp.dot(
        select, exclusive, precision=highest, preferred_element_type=jnp.float32
    )
    factors = jnp.where(
        (indices > position)[:, None],
        jnp.exp(jnp.minimum(exclusive_from - inclusive_mine[None, :], 0.0)),
        0.0,
    )
    later_grad = jnp.einsum("fh,fhpn->hpn", factors, pieces, precision=highest)
    gradients = pullback((grad_output, later_grad))
    grad_signal = gradients[0]
    grad_writer = gradients[1]
    grad_reader = gradients[2]
    grad_step = gradients[3]
    grad_bc = lax.psum_scatter(
        jnp.concatenate([grad_writer, grad_reader], axis=1), "dp", scatter_dimension=1, tiled=True
    )
    return (grad_signal.astype(jnp.bfloat16), grad_gating.astype(jnp.bfloat16), grad_bc, grad_step)


def solution(mesh):
    in_specs = (
        P("context", "dp"),
        P("context", "dp"),
        P("context", None),
        P("context", None),
        P("context", "dp"),
        P("dp"),
        P("dp"),
        P("dp"),
        P("context", "dp"),
    )
    out_specs = (P("context", "dp"), P("context", "dp"), P("context", "dp"), P("context", "dp"))
    return jax.shard_map(
        on_device, mesh=mesh, in_specs=in_specs, out_specs=out_specs, check_vma=False
    )
```

profile of v0, /device:TPU:0, one launch (start us, length us, event | category | flops | bytes accessed | tf_op | source)
XLA Modules:
  0.0 398.9 jit_solution(4576556629796148414)
XLA Ops:
  9.3 2.3 reduce-window.68
  15.5 1.8 fusion.106
  18.4 22.6 %all-gather.2 = f32[8,1,8]{2,1,0:T(1,128)S(1)} all-gather(f32[1,1,8]{2,1,0:T(1,128)S(1)} %bitcast.366), channel_id=1, replica_groups=mesh['dp'=4,'context'=8] {'context'}, dimensions={0}, use_global_device_ids=true | all-gather | bytes 288 | tf_op jit(solution)/shard_map/all_gather | solution.py:70
  41.3 1.7 copy.71
  45.0 1.9 copy.73
  47.6 21.7 %all-gather.6.cloned.1.call-done = f32[64,64,128]{2,1,0:T(8,128)} async-done(((f32[8,64,128]{2,1,0:T(8,128)}), f32[64,64,128]{2,1,0:T(8,128)}) %all-gather.6.cloned.1.call-update) | async-done | bytes 2097168 | tf_op jit(solution)/shard_map/all_gather | solution.py:78
  69.4 4.4 %fusion.102 = f32[8,1,64,128]{3,1,2,0:T(1,128)S(1)} fusion(f32[8,8,1,1]{0,2,3,1:T(1,128)S(1)} %copy.85, f32[8,8,64,128]{3,2,1,0:T(8,128)} %bitcast.349), kind=kOutput, calls=%fused_computation.142 | convolution fusion | flops 6291456 | bytes 2359552 | tf_op jit(solution)/shard_map/fh,fhpn->hpn/dot_general | solution.py:89
  73.8 92.1 %while.39 = (s32[]{:T(128)}, f32[8,64,128]{2,1,0:T(8,128)S(1)}, f32[4,256,8,64]{1,0,3,2:T(4,128)}, f32[4,8,64,128]{3,2,1,0:T(8,128)}, f32[4,256,8]{1,2,0:T(8,128...) while((s32[]{:T(128)}, f32[8,64,128]{2,1,0:T(8,128)S(1)}, ...), condition=%wide.region_6.7_spmd.clone, body=%wide.region_3.6_spmd.clone.sunk | while | flops 909158400 | bytes 7812925 | solution.py:49
  76.1 3.5 fusion.231
  79.6 1.7 fusion.232
  81.8 12.3 %dynamic_update_slice.68 = f32[4,256,8,64]{1,0,3,2:T(4,128)} dynamic-update-slice(f32[4,256,8,64]{1,0,3,2:T(4,128)} %get-tuple-element.828, f32[1,256,8,64]{1,0,3,2:T(1,128)S(1)} %copy.123, s32[]{:T(128)} %get-tuple-element.826, s32[]{:T(128)} %constant.134.clone.1..sunk, s32[]{:T(128)} %constant.134.clone.1..sunk, s32[]{:T(128)} %constant.134.clone.1..sunk) | dynamic-update-slice | bytes 1048580 | tf_op jit(solution)/shard_map/jvp()/while/body/jit(dynamic_update_index_in_dim)/dynamic_update_slice | solution.py:49
  95.1 1.7 convolution_add_fusion.7
  99.1 3.5 fusion.231
  102.6 1.7 fusion.232
  104.8 12.3 %dynamic_update_slice.68 = f32[4,256,8,64]{1,0,3,2:T(4,128)} dynamic-update-slice(f32[4,256,8,64]{1,0,3,2:T(4,128)} %get-tuple-element.828, f32[1,256,8,64]{1,0,3,2:T(1,128)S(1)} %copy.123, s32[]{:T(128)} %get-tuple-element.826, s32[]{:T(128)} %constant.134.clone.1..sunk, s32[]{:T(128)} %constant.134.clone.1..sunk, s32[]{:T(128)} %constant.134.clone.1..sunk) | dynamic-update-slice | bytes 1048580 | tf_op jit(solution)/shard_map/jvp()/while/body/jit(dynamic_update_index_in_dim)/dynamic_update_slice | solution.py:49
  118.2 1.7 convolution_add_fusion.7
  122.1 3.5 fusion.231
  127.9 12.3 %dynamic_update_slice.68 = f32[4,256,8,64]{1,0,3,2:T(4,128)} dynamic-update-slice(f32[4,256,8,64]{1,0,3,2:T(4,128)} %get-tuple-element.828, f32[1,256,8,64]{1,0,3,2:T(1,128)S(1)} %copy.123, s32[]{:T(128)} %get-tuple-element.826, s32[]{:T(128)} %constant.134.clone.1..sunk, s32[]{:T(128)} %constant.134.clone.1..sunk, s32[]{:T(128)} %constant.134.clone.1..sunk) | dynamic-update-slice | bytes 1048580 | tf_op jit(solution)/shard_map/jvp()/while/body/jit(dynamic_update_index_in_dim)/dynamic_update_slice | solution.py:49
  141.2 1.7 convolution_add_fusion.7
  145.2 3.5 fusion.231
  150.9 12.3 %dynamic_update_slice.68 = f32[4,256,8,64]{1,0,3,2:T(4,128)} dynamic-update-slice(f32[4,256,8,64]{1,0,3,2:T(4,128)} %get-tuple-element.828, f32[1,256,8,64]{1,0,3,2:T(1,128)S(1)} %copy.123, s32[]{:T(128)} %get-tuple-element.826, s32[]{:T(128)} %constant.134.clone.1..sunk, s32[]{:T(128)} %constant.134.clone.1..sunk, s32[]{:T(128)} %constant.134.clone.1..sunk) | dynamic-update-slice | bytes 1048580 | tf_op jit(solution)/shard_map/jvp()/while/body/jit(dynamic_update_index_in_dim)/dynamic_update_slice | solution.py:49
  164.2 1.7 convolution_add_fusion.7
  165.9 2.1 copy.104
  169.3 6.0 %all-reduce.2 = (f32[1024]{0:T(1024)S(1)}, f32[1024]{0:T(1024)S(1)}) all-reduce(f32[1024]{0:T(1024)S(1)} %get-tuple-element.523, f32[1024]{0:T(1024)S(1)} %get-tuple-element.522), channel_id=1, replica_groups=mesh['dp'=4,'context'=8] {'dp'}, use_global_device_ids=true, to_apply=%region_10.11 | all-reduce | flops 2048 | bytes 16384 | tf_op jit(solution)/shard_map/psum | solution.py:102
  175.3 4.6 %fusion.99 = (bf16[1024,512]{0,1:T(8,128)(2,1)}, f32[1024,512]{0,1:T(8,128)S(1)}) fusion(bf16[1024,512]{0,1:T(8,128)(2,1)} %copy-done.2, f32[1024,512]{0,1:T(8,128)} %bitcast.347, bf16[1024,512]{0,1:T(8,128)(2,1)} %copy-done.1, f32[1024]{0:T(1024)S(1)} %get-tuple-element.597, f32[1024]{0:T(1024)S(1)} %get-tuple-element.596, f32[512]{0:T(512)S(1)} %copy-done.16), kind=kLoop, calls=%fused_computation.139 | loop fusion | flops 9961472 | bytes 7350272 | tf_op jit(solution)/shard_map/convert_element_type | solution.py:141
  179.9 1.8 fusion.104
  182.1 2.0 reshape.256
  184.1 45.7 %all-gather.8.cloned.1.call-done = f32[64,64,128]{2,1,0:T(8,128)} async-done(((f32[8,64,128]{2,1,0:T(8,128)}), f32[64,64,128]{2,1,0:T(8,128)}) %all-gather.8.cloned.1.call-update) | async-done | bytes 2097168 | tf_op jit(solution)/shard_map/all_gather | solution.py:121
  229.8 4.4 %fusion.100 = f32[8,1,64,128]{3,1,2,0:T(1,128)S(1)} fusion(f32[8,8,1,1]{0,2,3,1:T(1,128)S(1)} %copy.88, f32[8,8,64,128]{3,2,1,0:T(8,128)} %bitcast.350), kind=kOutput, calls=%fused_computation.140 | convolution fusion | flops 6291456 | bytes 2359552 | tf_op jit(solution)/shard_map/fh,fhpn->hpn/dot_general | solution.py:132
  237.7 127.6 %while.38 = (s32[]{:T(128)}, f32[8,64,128]{2,1,0:T(8,128)S(1)}, bf16[4,256,8,64]{1,3,2,0:T(8,128)(2,1)}, f32[4,256,128]{2,1,0:T(8,128)}, f32[4,256,128]{2,1,0:T(...) while((s32[]{:T(128)}, f32[8,64,128]{2,1,0:T(8,128)S(1)}, ...), condition=%wide.region_23.24_spmd, body=%wide.region_11.23_spmd.sunk | while | flops 2125232128 | bytes 24865956 | solution.py:49
  237.7 2.1 constant_dynamic-slice_fusion.2
  247.7 4.0 %fusion.215 = (f32[256,8]{0,1:T(8,128)}, f32[256,8]{0,1:T(8,128)}, f32[256,8]{0,1:T(8,128)}, f32[256,256]{1,0:T(8,128)S(1)}) fusion(f32[256,8]{0,1:T(8,128)S(1)} %get-tuple-element.788, f32[256,8]{0,1:T(8,128)S(1)} %get-tuple-element.783, f32[256,256]{1,0:T(8,128)S(1)} %fusion.214, pred[256,256]{1,0:T(8,128)(4,1)S(1)} %iota_compare_fusion.8, ...), kind=kOutput, calls=%fused_computation.66.clone.1 | convolution fusion | flops 409397248 | bytes 1679360 | tf_op jit(solution)/shard_map/transpose(jvp())/while/body/eval_jaxpr/checkpoint/tsh,shp->thp/dot_general | solution.py:27
  253.8 3.1 reduce-window.80
  265.3 2.6 fusion.217
  269.6 2.1 constant_dynamic-slice_fusion.2
  279.6 4.0 %fusion.215 = (f32[256,8]{0,1:T(8,128)}, f32[256,8]{0,1:T(8,128)}, f32[256,8]{0,1:T(8,128)}, f32[256,256]{1,0:T(8,128)S(1)}) fusion(f32[256,8]{0,1:T(8,128)S(1)} %get-tuple-element.788, f32[256,8]{0,1:T(8,128)S(1)} %get-tuple-element.783, f32[256,256]{1,0:T(8,128)S(1)} %fusion.214, pred[256,256]{1,0:T(8,128)(4,1)S(1)} %iota_compare_fusion.8, ...), kind=kOutput, calls=%fused_computation.66.clone.1 | convolution fusion | flops 409397248 | bytes 1679360 | tf_op jit(solution)/shard_map/transpose(jvp())/while/body/eval_jaxpr/checkpoint/tsh,shp->thp/dot_general | solution.py:27
  285.7 3.1 reduce-window.80
  297.2 2.6 fusion.217
  301.5 2.1 constant_dynamic-slice_fusion.2
  311.5 4.0 %fusion.215 = (f32[256,8]{0,1:T(8,128)}, f32[256,8]{0,1:T(8,128)}, f32[256,8]{0,1:T(8,128)}, f32[256,256]{1,0:T(8,128)S(1)}) fusion(f32[256,8]{0,1:T(8,128)S(1)} %get-tuple-element.788, f32[256,8]{0,1:T(8,128)S(1)} %get-tuple-element.783, f32[256,256]{1,0:T(8,128)S(1)} %fusion.214, pred[256,256]{1,0:T(8,128)(4,1)S(1)} %iota_compare_fusion.8, ...), kind=kOutput, calls=%fused_computation.66.clone.1 | convolution fusion | flops 409397248 | bytes 1679360 | tf_op jit(solution)/shard_map/transpose(jvp())/while/body/eval_jaxpr/checkpoint/tsh,shp->thp/dot_general | solution.py:27
  317.6 3.1 reduce-window.80
  329.1 2.6 fusion.217
  333.4 2.1 constant_dynamic-slice_fusion.2
  343.4 4.0 %fusion.215 = (f32[256,8]{0,1:T(8,128)}, f32[256,8]{0,1:T(8,128)}, f32[256,8]{0,1:T(8,128)}, f32[256,256]{1,0:T(8,128)S(1)}) fusion(f32[256,8]{0,1:T(8,128)S(1)} %get-tuple-element.788, f32[256,8]{0,1:T(8,128)S(1)} %get-tuple-element.783, f32[256,256]{1,0:T(8,128)S(1)} %fusion.214, pred[256,256]{1,0:T(8,128)(4,1)S(1)} %iota_compare_fusion.8, ...), kind=kOutput, calls=%fused_computation.66.clone.1 | convolution fusion | flops 409397248 | bytes 1679360 | tf_op jit(solution)/shard_map/transpose(jvp())/while/body/eval_jaxpr/checkpoint/tsh,shp->thp/dot_general | solution.py:27
  349.5 3.1 reduce-window.80
  361.0 2.6 fusion.217
  371.5 2.0 reshape.292
  373.6 18.8 %reduce-scatter.2.cloned.1.call-done = f32[1024,64]{0,1:T(8,128)} async-done(((f32[1024,256]{0,1:T(8,128)}), f32[1024,64]{0,1:T(8,128)}) %reduce-scatter.2.cloned.1.call-update) | async-done | bytes 262160 | tf_op jit(solution)/shard_map/reduce_scatter | solution.py:138
  (287 shorter events, 119.2 us)
Async XLA Ops:
  7.2 62.2 %all-gather.6.cloned.1.call-start = ((), (), s32[]{:S(2)}) async-start(), calls=%async_computation.2 | async-start | bytes 2359296 | tf_op jit(solution)/shard_map/all_gather | solution.py:78
  14.5 1.0 copy-start.9
  17.3 212.5 %all-gather.8.cloned.1.call-start = ((), (), s32[]{:S(2)}) async-start(), calls=%async_computation.3 | async-start | bytes 2359296 | tf_op jit(solution)/shard_map/all_gather | solution.py:121
  41.3 1.8 copy-start.10
  43.0 1.4 copy-start.8
  45.0 123.0 %copy-start.1 = (bf16[1024,512]{0,1:T(8,128)(2,1)}, bf16[1024,512]{0,1:T(8,128)(2,1)S(1)}, u32[]{:S(2)}) copy-start(bf16[1024,512]{0,1:T(8,128)(2,1)S(1)} %copy.69) | copy-start | bytes 3145732
  45.0 28.8 %copy-start.7 = (f32[1024,8]{0,1:T(8,128)S(1)}, f32[1024,8]{0,1:T(8,128)}, u32[]{:S(2)}) copy-start(f32[1024,8]{0,1:T(8,128)} %param.17) | copy-start | bytes 98308
  46.9 121.1 %copy-start.2 = (bf16[1024,512]{0,1:T(8,128)(2,1)}, bf16[1024,512]{0,1:T(8,128)(2,1)S(1)}, u32[]{:S(2)}) copy-start(bf16[1024,512]{0,1:T(8,128)(2,1)S(1)} %copy.73) | copy-start | bytes 3145732
  165.9 2.1 copy-start.16
  168.0 1.3 copy-start
  175.3 4.6 %copy-start.11 = (bf16[1024,128]{1,0:T(8,128)(2,1)S(1)}, bf16[1024,128]{1,0:T(8,128)(2,1)}, u32[]{:S(2)}) copy-start(bf16[1024,128]{1,0:T(8,128)(2,1)} %param.16) | copy-start | bytes 786436
  181.8 210.6 %reduce-scatter.2.cloned.1.call-start = ((), (), s32[]{:S(2)}) async-start(), calls=%async_computation.1 | async-start | bytes 1310720 | tf_op jit(solution)/shard_map/reduce_scatter | solution.py:138
  247.1 0.6 copy-start.12
  247.6 4.1 %copy-start.14 = (f32[256,8]{0,1:T(8,128)}, f32[256,8]{0,1:T(8,128)S(1)}, u32[]{:S(2)}) copy-start(f32[256,8]{0,1:T(8,128)S(1)} %get-tuple-element.788) | copy-start | bytes 24580 | tf_op jit(solution)/shard_map/transpose(jvp())/while
  258.8 6.4 %copy-start.4 = (bf16[4,256,8,64]{1,3,2,0:T(8,128)(2,1)S(1)}, bf16[4,256,8,64]{1,3,2,0:T(8,128)(2,1)}, u32[]{:S(2)}) copy-start(bf16[4,256,8,64]{1,3,2,0:T(8,128)(2,1)} %get-tuple-element.873) | copy-start | bytes 3145732 | tf_op jit(solution)/shard_map/transpose(jvp())/while
  258.8 6.4 %copy-start.15 = (f32[256,8]{0,1:T(8,128)S(1)}, f32[256,8]{0,1:T(8,128)}, u32[]{:S(2)}) copy-start(f32[256,8]{0,1:T(8,128)} %copy-done.14) | copy-start | bytes 24580 | tf_op jit(solution)/shard_map/transpose(jvp())/while
  265.3 3.6 copy-start.13
  267.9 1.0 copy-start.5
  279.0 0.6 copy-start.12
  279.5 4.1 %copy-start.14 = (f32[256,8]{0,1:T(8,128)}, f32[256,8]{0,1:T(8,128)S(1)}, u32[]{:S(2)}) copy-start(f32[256,8]{0,1:T(8,128)S(1)} %get-tuple-element.788) | copy-start | bytes 24580 | tf_op jit(solution)/shard_map/transpose(jvp())/while
  290.7 6.5 %copy-start.4 = (bf16[4,256,8,64]{1,3,2,0:T(8,128)(2,1)S(1)}, bf16[4,256,8,64]{1,3,2,0:T(8,128)(2,1)}, u32[]{:S(2)}) copy-start(bf16[4,256,8,64]{1,3,2,0:T(8,128)(2,1)} %get-tuple-element.873) | copy-start | bytes 3145732 | tf_op jit(solution)/shard_map/transpose(jvp())/while
  290.7 6.5 %copy-start.15 = (f32[256,8]{0,1:T(8,128)S(1)}, f32[256,8]{0,1:T(8,128)}, u32[]{:S(2)}) copy-start(f32[256,8]{0,1:T(8,128)} %copy-done.14) | copy-start | bytes 24580 | tf_op jit(solution)/shard_map/transpose(jvp())/while
  297.2 3.6 copy-start.13
  299.8 1.0 copy-start.5
  310.9 0.6 copy-start.12
  311.5 4.1 %copy-start.14 = (f32[256,8]{0,1:T(8,128)}, f32[256,8]{0,1:T(8,128)S(1)}, u32[]{:S(2)}) copy-start(f32[256,8]{0,1:T(8,128)S(1)} %get-tuple-element.788) | copy-start | bytes 24580 | tf_op jit(solution)/shard_map/transpose(jvp())/while
  322.7 6.4 %copy-start.4 = (bf16[4,256,8,64]{1,3,2,0:T(8,128)(2,1)S(1)}, bf16[4,256,8,64]{1,3,2,0:T(8,128)(2,1)}, u32[]{:S(2)}) copy-start(bf16[4,256,8,64]{1,3,2,0:T(8,128)(2,1)} %get-tuple-element.873) | copy-start | bytes 3145732 | tf_op jit(solution)/shard_map/transpose(jvp())/while
  322.7 6.4 %copy-start.15 = (f32[256,8]{0,1:T(8,128)S(1)}, f32[256,8]{0,1:T(8,128)}, u32[]{:S(2)}) copy-start(f32[256,8]{0,1:T(8,128)} %copy-done.14) | copy-start | bytes 24580 | tf_op jit(solution)/shard_map/transpose(jvp())/while
  329.1 3.6 copy-start.13
  331.7 1.0 copy-start.5
  342.8 0.6 copy-start.12
  343.4 4.1 %copy-start.14 = (f32[256,8]{0,1:T(8,128)}, f32[256,8]{0,1:T(8,128)S(1)}, u32[]{:S(2)}) copy-start(f32[256,8]{0,1:T(8,128)S(1)} %get-tuple-element.788) | copy-start | bytes 24580 | tf_op jit(solution)/shard_map/transpose(jvp())/while
  354.6 6.4 %copy-start.4 = (bf16[4,256,8,64]{1,3,2,0:T(8,128)(2,1)S(1)}, bf16[4,256,8,64]{1,3,2,0:T(8,128)(2,1)}, u32[]{:S(2)}) copy-start(bf16[4,256,8,64]{1,3,2,0:T(8,128)(2,1)} %get-tuple-element.873) | copy-start | bytes 3145732 | tf_op jit(solution)/shard_map/transpose(jvp())/while
  354.6 6.4 %copy-start.15 = (f32[256,8]{0,1:T(8,128)S(1)}, f32[256,8]{0,1:T(8,128)}, u32[]{:S(2)}) copy-start(f32[256,8]{0,1:T(8,128)} %copy-done.14) | copy-start | bytes 24580 | tf_op jit(solution)/shard_map/transpose(jvp())/while
  361.0 3.6 copy-start.13
  363.6 1.0 copy-start.5
  366.5 2.4 copy-start.3
  368.9 1.4 copy-start.6
Sparse Core Ops, SparseCore 0:
  17.4 51.8 all-gather.5
  181.9 47.9 all-gather.7
  369.1 23.2 reduce-scatter.1
where the time goes:
time: 402 us; the launch traced here: 399 us
  local copies, waits for them, and re-layouts  115 us (29%)
  matrix products  98.3 us (24%)
  waiting for transfers between devices  86.3 us (21%)
  other arithmetic  56.4 us (14%)
  blocking collectives  28.5 us (7%)
  between operations  14 us (3%)
    dynamic_update_slice x12, local copies, waits for them, and re-layouts, recurrence(): end_state, outputs = lax.scan(advance, start_state, pieces)  54.4 us
    all_gather x1, waiting for transfers between devices, on_device(): pieces = lax.all_gather(influence[None], 'context', axis=0, tiled=True)  45.7 us
    dot_general x12, matrix products, block_step(): within = jnp.einsum('tsh,shp->thp', mixing, signal_block, precision=highest)  40.6 us
    another operation x40, other arithmetic  34.5 us
    all_gather x1, blocking collectives, on_device(): all_totals = lax.all_gather(totals[None, :], 'context', axis=0, tiled=True)  22.6 us
    all_gather x1, waiting for transfers between devices, on_device(): pieces = lax.all_gather(local_end[None], 'context', axis=0, tiled=True)  21.7 us
    reduce_scatter x1, waiting for transfers between devices, on_device(): lax.psum_scatter(jnp.concatenate([grad_writer, grad_reader], axis=1), 'dp...  18.8 us
    dot_general x16, matrix products, block_step(): jnp.dot(reader_block, writer_block.T, precision=highest, preferred_elemen...  15.9 us
  transfers between devices with their start and end apart: 3, of which 3 were waited for; matrix products, arithmetic and copies ran while one was open for 3% of the time, Pallas kernels for 0%

commit v1 on v0

--- a/solution.py
+++ b/solution.py
@@ -118,7 +118,14 @@
         reader_f,
         precision=highest,
     )
-    pieces = lax.all_gather(influence[None], "context", axis=0, tiled=True)
+    ring = [influence[None]]
+    for hop in range(7):
+        ring.append(lax.ppermute(ring[-1], "context", [(dev, (dev + 1) % 8) for dev in range(8)]))
+    pieces = jnp.roll(
+        jnp.concatenate(ring[::-1], axis=0),
+        (lax.axis_index("context") + 1) * ring[0].shape[0],
+        axis=0,
+    )
     indices = jnp.arange(pieces.shape[0])
     select = (indices[:, None] == jnp.arange(devices)[None, :]).astype(jnp.float32)
     exclusive_from = jnp.dot(

time: 402 us -> 397 us (0.988)
  other arithmetic: 56.4 us -> 38.5 us
  waiting for transfers between devices: 86.3 us -> 101 us
  matrix products: 98.3 us -> 92.2 us
    ppermute x0 -> x7, waiting for transfers between devices: none -> 64.4 us  [on_device(): lax.ppermute(ring[-1], 'context', [(dev, (dev + 1) % 8) for dev in range(...]
    all_gather x1 -> x0, waiting for transfers between devices: 45.7 us -> none  [on_device(): pieces = lax.all_gather(influence[None], 'context', axis=0, tiled=True)]
    unnamed x31 -> x62, local copies, waits for them, and re-layouts: 13.8 us -> 26.9 us
    another operation x40, other arithmetic: 34.5 us -> 22.3 us
    another operation x29, local copies, waits for them, and re-layouts: 9.94 us -> 4.63 us
    while x48 -> x88, local copies, waits for them, and re-layouts: 5.45 us -> 0.18 us
  transfers between devices with their start and end apart: 3 -> 9, of which waited for: 3 -> 9; matrix products, arithmetic and copies ran while one was open for 3% -> 4% of each run, Pallas kernels for 0% -> 0%
where the time goes in v1:
time: 397 us; the launch traced here: 394 us
  local copies, waits for them, and re-layouts  118 us (30%)
  waiting for transfers between devices  101 us (25%)
  matrix products  92.2 us (23%)
  other arithmetic  38.5 us (10%)
  blocking collectives  28.5 us (7%)
  between operations  14.5 us (4%)
    ppermute x7, waiting for transfers between devices, on_device(): lax.ppermute(ring[-1], 'context', [(dev, (dev + 1) % 8) for dev in range(...  64.4 us
    dynamic_update_slice x12, local copies, waits for them, and re-layouts, recurrence(): end_state, outputs = lax.scan(advance, start_state, pieces)  54.3 us
    dot_general x12, matrix products, block_step(): within = jnp.einsum('tsh,shp->thp', mixing, signal_block, precision=highest)  40.4 us
    unnamed x62, local copies, waits for them, and re-layouts  26.9 us
    all_gather x1, blocking collectives, on_device(): all_totals = lax.all_gather(totals[None, :], 'context', axis=0, tiled=True)  22.6 us
    another operation x40, other arithmetic  22.3 us
    all_gather x1, waiting for transfers between devices, on_device(): pieces = lax.all_gather(local_end[None], 'context', axis=0, tiled=True)  19.8 us
    reduce_scatter x1, waiting for transfers between devices, on_device(): lax.psum_scatter(jnp.concatenate([grad_writer, grad_reader], axis=1), 'dp...  16.6 us
  transfers between devices with their start and end apart: 9, of which 9 were waited for; matrix products, arithmetic and copies ran while one was open for 4% of the time, Pallas kernels for 0%

profile of v1, /device:TPU:0, one launch (start us, length us, event | category | flops | bytes accessed | tf_op | source)
XLA Modules:
  0.0 394.1 jit_solution(7314883328121997693)
XLA Ops:
  8.7 2.3 reduce-window.68
  16.0 1.9 reshape.262
  19.4 22.6 %all-gather.1 = f32[8,1,8]{2,1,0:T(1,128)S(1)} all-gather(f32[1,1,8]{2,1,0:T(1,128)S(1)} %bitcast.369), channel_id=1, replica_groups=mesh['dp'=4,'context'=8] {'context'}, dimensions={0}, use_global_device_ids=true | all-gather | bytes 288 | tf_op jit(solution)/shard_map/all_gather | solution.py:70
  42.3 3.4 copy.71
  45.8 2.3 copy.69
  48.1 19.8 %all-gather.4.cloned.1.call-done = f32[64,64,128]{2,1,0:T(8,128)} async-done(((f32[8,64,128]{2,1,0:T(8,128)}), f32[64,64,128]{2,1,0:T(8,128)}) %all-gather.4.cloned.1.call-update) | async-done | bytes 2097168 | tf_op jit(solution)/shard_map/all_gather | solution.py:78
  67.9 4.4 %fusion.102 = f32[8,1,64,128]{3,1,2,0:T(1,128)S(1)} fusion(f32[8,8,1,1]{0,2,3,1:T(1,128)S(1)} %copy.85, f32[8,8,64,128]{3,2,1,0:T(8,128)} %bitcast.350), kind=kOutput, calls=%fused_computation.142 | convolution fusion | flops 6291456 | bytes 2359552 | tf_op jit(solution)/shard_map/fh,fhpn->hpn/dot_general | solution.py:89
  72.3 88.4 %while.39 = (s32[]{:T(128)}, f32[8,64,128]{2,1,0:T(8,128)S(1)}, f32[4,256,8,64]{1,0,3,2:T(4,128)}, f32[4,8,64,128]{3,2,1,0:T(8,128)}, f32[4,256,8]{1,2,0:T(8,128...) while((s32[]{:T(128)}, f32[8,64,128]{2,1,0:T(8,128)S(1)}, ...), condition=%wide.region_6.7_spmd.clone, body=%wide.region_3.6_spmd.clone.sunk | while | flops 909158400 | bytes 7811437 | solution.py:49
  74.4 3.5 fusion.234
  82.1 12.3 %dynamic_update_slice.68 = f32[4,256,8,64]{1,0,3,2:T(4,128)} dynamic-update-slice(f32[4,256,8,64]{1,0,3,2:T(4,128)} %get-tuple-element.828, f32[1,256,8,64]{1,0,3,2:T(1,128)S(1)} %copy.123, s32[]{:T(128)S(6)} %copy.134, s32[]{:T(128)} %constant.153.clone.1..sunk, s32[]{:T(128)} %constant.153.clone.1..sunk, s32[]{:T(128)} %constant.153.clone.1..sunk) | dynamic-update-slice | bytes 1048580 | tf_op jit(solution)/shard_map/jvp()/while/body/jit(dynamic_update_index_in_dim)/dynamic_update_slice | solution.py:49
  96.5 3.5 fusion.234
  104.2 12.3 %dynamic_update_slice.68 = f32[4,256,8,64]{1,0,3,2:T(4,128)} dynamic-update-slice(f32[4,256,8,64]{1,0,3,2:T(4,128)} %get-tuple-element.828, f32[1,256,8,64]{1,0,3,2:T(1,128)S(1)} %copy.123, s32[]{:T(128)S(6)} %copy.134, s32[]{:T(128)} %constant.153.clone.1..sunk, s32[]{:T(128)} %constant.153.clone.1..sunk, s32[]{:T(128)} %constant.153.clone.1..sunk) | dynamic-update-slice | bytes 1048580 | tf_op jit(solution)/shard_map/jvp()/while/body/jit(dynamic_update_index_in_dim)/dynamic_update_slice | solution.py:49
  118.6 3.5 fusion.234
  126.3 12.3 %dynamic_update_slice.68 = f32[4,256,8,64]{1,0,3,2:T(4,128)} dynamic-update-slice(f32[4,256,8,64]{1,0,3,2:T(4,128)} %get-tuple-element.828, f32[1,256,8,64]{1,0,3,2:T(1,128)S(1)} %copy.123, s32[]{:T(128)S(6)} %copy.134, s32[]{:T(128)} %constant.153.clone.1..sunk, s32[]{:T(128)} %constant.153.clone.1..sunk, s32[]{:T(128)} %constant.153.clone.1..sunk) | dynamic-update-slice | bytes 1048580 | tf_op jit(solution)/shard_map/jvp()/while/body/jit(dynamic_update_index_in_dim)/dynamic_update_slice | solution.py:49
  140.7 3.5 fusion.234
  148.4 12.3 %dynamic_update_slice.68 = f32[4,256,8,64]{1,0,3,2:T(4,128)} dynamic-update-slice(f32[4,256,8,64]{1,0,3,2:T(4,128)} %get-tuple-element.828, f32[1,256,8,64]{1,0,3,2:T(1,128)S(1)} %copy.123, s32[]{:T(128)S(6)} %copy.134, s32[]{:T(128)} %constant.153.clone.1..sunk, s32[]{:T(128)} %constant.153.clone.1..sunk, s32[]{:T(128)} %constant.153.clone.1..sunk) | dynamic-update-slice | bytes 1048580 | tf_op jit(solution)/shard_map/jvp()/while/body/jit(dynamic_update_index_in_dim)/dynamic_update_slice | solution.py:49
  160.7 2.1 copy.104
  164.1 6.0 %all-reduce.2 = (f32[1024]{0:T(1024)S(1)}, f32[1024]{0:T(1024)S(1)}) all-reduce(f32[1024]{0:T(1024)S(1)} %get-tuple-element.523, f32[1024]{0:T(1024)S(1)} %get-tuple-element.522), channel_id=1, replica_groups=mesh['dp'=4,'context'=8] {'dp'}, use_global_device_ids=true, to_apply=%region_10.11 | all-reduce | flops 2048 | bytes 16384 | tf_op jit(solution)/shard_map/psum | solution.py:102
  170.1 4.6 %fusion.99 = (bf16[1024,512]{0,1:T(8,128)(2,1)}, f32[1024,512]{0,1:T(8,128)S(1)}) fusion(bf16[1024,512]{0,1:T(8,128)(2,1)} %copy-done.3, f32[1024,512]{0,1:T(8,128)} %bitcast.348, bf16[1024,512]{0,1:T(8,128)(2,1)} %copy.69, f32[1024]{0:T(1024)S(1)} %get-tuple-element.597, f32[1024]{0:T(1024)S(1)} %get-tuple-element.596, f32[512]{0:T(512)S(1)} %copy-done.29), kind=kLoop, calls=%fused_computation.139 | loop fusion | flops 9961472 | bytes 7350272 | tf_op jit(solution)/shard_map/convert_element_type | solution.py:148
  176.5 10.2 %collective-permute-done = f32[1,8,64,128]{3,2,1,0:T(8,128)S(1)} collective-permute-done((f32[1,8,64,128]{3,2,1,0:T(8,128)S(1)}, f32[1,8,64,128]{3,2,1,0:T(8,128)S(1)}, u32[]{:S(2)}, u32[]{:S(2)}) %collective-permute-start) | collective-permute-done | bytes 262176 | tf_op jit(solution)/shard_map/ppermute | solution.py:123
  187.4 9.9 %collective-permute-done.1 = f32[1,8,64,128]{3,2,1,0:T(8,128)S(1)} collective-permute-done((f32[1,8,64,128]{3,2,1,0:T(8,128)S(1)}, f32[1,8,64,128]{3,2,1,0:T(8,128)S(1)}, u32[]{:S(2)}, u32[]{:S(2)}) %collective-permute-start.1) | collective-permute-done | bytes 262176 | tf_op jit(solution)/shard_map/ppermute | solution.py:123
  198.1 9.1 %collective-permute-done.2 = f32[1,8,64,128]{3,2,1,0:T(8,128)S(1)} collective-permute-done((f32[1,8,64,128]{3,2,1,0:T(8,128)S(1)}, f32[1,8,64,128]{3,2,1,0:T(8,128)S(1)}, u32[]{:S(2)}, u32[]{:S(2)}) %collective-permute-start.2) | collective-permute-done | bytes 262176 | tf_op jit(solution)/shard_map/ppermute | solution.py:123
  207.8 9.1 %collective-permute-done.3 = f32[1,8,64,128]{3,2,1,0:T(8,128)S(1)} collective-permute-done((f32[1,8,64,128]{3,2,1,0:T(8,128)S(1)}, f32[1,8,64,128]{3,2,1,0:T(8,128)S(1)}, u32[]{:S(2)}, u32[]{:S(2)}) %collective-permute-start.3) | collective-permute-done | bytes 262176 | tf_op jit(solution)/shard_map/ppermute | solution.py:123
  217.6 9.1 %collective-permute-done.4 = f32[1,8,64,128]{3,2,1,0:T(8,128)S(1)} collective-permute-done((f32[1,8,64,128]{3,2,1,0:T(8,128)S(1)}, f32[1,8,64,128]{3,2,1,0:T(8,128)S(1)}, u32[]{:S(2)}, u32[]{:S(2)}) %collective-permute-start.4) | collective-permute-done | bytes 262176 | tf_op jit(solution)/shard_map/ppermute | solution.py:123
  227.4 10.0 %collective-permute-done.5 = f32[1,8,64,128]{3,2,1,0:T(8,128)} collective-permute-done((f32[1,8,64,128]{3,2,1,0:T(8,128)S(1)}, f32[1,8,64,128]{3,2,1,0:T(8,128)}, u32[]{:S(2)}, u32[]{:S(2)}) %collective-permute-start.5) | collective-permute-done | bytes 262176 | tf_op jit(solution)/shard_map/ppermute | solution.py:123
  237.7 2.0 reshape.256
  239.7 7.1 %collective-permute-done.6 = f32[1,8,64,128]{3,2,1,0:T(8,128)} collective-permute-done((f32[1,8,64,128]{3,2,1,0:T(8,128)}, f32[1,8,64,128]{3,2,1,0:T(8,128)}, u32[]{:S(2)}, u32[]{:S(2)}) %collective-permute-start.6) | collective-permute-done | bytes 262176 | tf_op jit(solution)/shard_map/ppermute | solution.py:123
  253.3 2.9 fusion.100
  259.6 101.8 %while.38 = (s32[]{:T(128)}, f32[8,64,128]{2,1,0:T(8,128)S(1)}, bf16[4,256,8,64]{1,3,2,0:T(8,128)(2,1)}, f32[4,256,128]{2,1,0:T(8,128)}, f32[4,256,128]{2,1,0:T(...) while((s32[]{:T(128)}, f32[8,64,128]{2,1,0:T(8,128)S(1)}, ...), condition=%wide.region_23.24_spmd, body=%wide.region_11.23_spmd.sunk | while | flops 2125232128 | bytes 29092472 | solution.py:49
  260.7 2.1 constant_dynamic-slice_fusion.3
  267.3 4.0 %fusion.218 = (f32[256,8]{0,1:T(8,128)}, f32[256,8]{0,1:T(8,128)}, f32[256,8]{0,1:T(8,128)}, f32[256,256]{1,0:T(8,128)S(1)}) fusion(f32[256,8]{0,1:T(8,128)S(1)} %get-tuple-element.788, f32[256,8]{0,1:T(8,128)S(1)} %get-tuple-element.783, f32[256,256]{1,0:T(8,128)S(1)} %fusion.217, pred[256,256]{1,0:T(8,128)(4,1)S(1)} %iota_compare_fusion.8, ...), kind=kOutput, calls=%fused_computation.66.clone.1 | convolution fusion | flops 409397248 | bytes 1679360 | tf_op jit(solution)/shard_map/transpose(jvp())/while/body/eval_jaxpr/checkpoint/tsh,shp->thp/dot_general | solution.py:27
  275.8 2.6 fusion.220
  281.7 2.5 reduce-window.80
  286.2 2.1 constant_dynamic-slice_fusion.3
  292.7 4.0 %fusion.218 = (f32[256,8]{0,1:T(8,128)}, f32[256,8]{0,1:T(8,128)}, f32[256,8]{0,1:T(8,128)}, f32[256,256]{1,0:T(8,128)S(1)}) fusion(f32[256,8]{0,1:T(8,128)S(1)} %get-tuple-element.788, f32[256,8]{0,1:T(8,128)S(1)} %get-tuple-element.783, f32[256,256]{1,0:T(8,128)S(1)} %fusion.217, pred[256,256]{1,0:T(8,128)(4,1)S(1)} %iota_compare_fusion.8, ...), kind=kOutput, calls=%fused_computation.66.clone.1 | convolution fusion | flops 409397248 | bytes 1679360 | tf_op jit(solution)/shard_map/transpose(jvp())/while/body/eval_jaxpr/checkpoint/tsh,shp->thp/dot_general | solution.py:27
  301.2 2.6 fusion.220
  307.2 2.5 reduce-window.80
  311.6 2.1 constant_dynamic-slice_fusion.3
  318.2 4.0 %fusion.218 = (f32[256,8]{0,1:T(8,128)}, f32[256,8]{0,1:T(8,128)}, f32[256,8]{0,1:T(8,128)}, f32[256,256]{1,0:T(8,128)S(1)}) fusion(f32[256,8]{0,1:T(8,128)S(1)} %get-tuple-element.788, f32[256,8]{0,1:T(8,128)S(1)} %get-tuple-element.783, f32[256,256]{1,0:T(8,128)S(1)} %fusion.217, pred[256,256]{1,0:T(8,128)(4,1)S(1)} %iota_compare_fusion.8, ...), kind=kOutput, calls=%fused_computation.66.clone.1 | convolution fusion | flops 409397248 | bytes 1679360 | tf_op jit(solution)/shard_map/transpose(jvp())/while/body/eval_jaxpr/checkpoint/tsh,shp->thp/dot_general | solution.py:27
  326.7 2.6 fusion.220
  332.6 2.5 reduce-window.80
  337.1 2.1 constant_dynamic-slice_fusion.3
  343.6 4.0 %fusion.218 = (f32[256,8]{0,1:T(8,128)}, f32[256,8]{0,1:T(8,128)}, f32[256,8]{0,1:T(8,128)}, f32[256,256]{1,0:T(8,128)S(1)}) fusion(f32[256,8]{0,1:T(8,128)S(1)} %get-tuple-element.788, f32[256,8]{0,1:T(8,128)S(1)} %get-tuple-element.783, f32[256,256]{1,0:T(8,128)S(1)} %fusion.217, pred[256,256]{1,0:T(8,128)(4,1)S(1)} %iota_compare_fusion.8, ...), kind=kOutput, calls=%fused_computation.66.clone.1 | convolution fusion | flops 409397248 | bytes 1679360 | tf_op jit(solution)/shard_map/transpose(jvp())/while/body/eval_jaxpr/checkpoint/tsh,shp->thp/dot_general | solution.py:27
  352.1 2.6 fusion.220
  358.0 2.5 reduce-window.80
  366.4 2.2 copy.91
  368.6 2.0 reshape.291
  370.7 16.6 %reduce-scatter.2.cloned.1.call-done = f32[1024,64]{0,1:T(8,128)} async-done(((f32[1024,256]{0,1:T(8,128)}), f32[1024,64]{0,1:T(8,128)}) %reduce-scatter.2.cloned.1.call-update) | async-done | bytes 262160 | tf_op jit(solution)/shard_map/reduce_scatter | solution.py:145
  (371 shorter events, 111.0 us)
Async XLA Ops:
  7.2 60.7 %all-gather.4.cloned.1.call-start = ((), (), s32[]{:S(2)}) async-start(), calls=%async_computation.2 | async-start | bytes 2359296 | tf_op jit(solution)/shard_map/all_gather | solution.py:78
  15.9 371.3 %reduce-scatter.2.cloned.1.call-start = ((), (), s32[]{:S(2)}) async-start(), calls=%async_computation.1 | async-start | bytes 1310720 | tf_op jit(solution)/shard_map/reduce_scatter | solution.py:145
  19.4 143.5 %copy-start.3 = (bf16[1024,512]{0,1:T(8,128)(2,1)}, bf16[1024,512]{0,1:T(8,128)(2,1)S(1)}, u32[]{:S(2)}) copy-start(bf16[1024,512]{0,1:T(8,128)(2,1)S(1)} %copy.73) | copy-start | bytes 3145732
  42.3 3.4 copy-start.20
  170.1 4.6 %copy-start.21 = (bf16[1024,128]{1,0:T(8,128)(2,1)S(1)}, bf16[1024,128]{1,0:T(8,128)(2,1)}, u32[]{:S(2)}) copy-start(bf16[1024,128]{1,0:T(8,128)(2,1)} %param.16) | copy-start | bytes 786436
  175.9 10.8 %collective-permute-start = (f32[1,8,64,128]{3,2,1,0:T(8,128)S(1)}, f32[1,8,64,128]{3,2,1,0:T(8,128)S(1)}, u32[]{:S(2)}, u32[]{:S(2)}) collective-permute-start(f32[1,8,64,128]{3,2,1,0:T(8,128)S(1)} %fusion.108), channel_id=1, source_target_pairs={{0,1},{1,2},{2,3},{3,4},{4,5},{5,6},{6,7},{7,0},{8,9},{9,10},{10,1... | collective-permute-start | bytes 786440 | tf_op jit(solution)/shard_map/ppermute | solution.py:123
  187.4 9.9 %collective-permute-start.1 = (f32[1,8,64,128]{3,2,1,0:T(8,128)S(1)}, f32[1,8,64,128]{3,2,1,0:T(8,128)S(1)}, u32[]{:S(2)}, u32[]{:S(2)}) collective-permute-start(f32[1,8,64,128]{3,2,1,0:T(8,128)S(1)} %collective-permute-done), channel_id=1, source_target_pairs={{0,1},{1,2},{2,3},{3,4},{4,5},{5,6},{6,7},{7,0},{8,9},{9,10},{10,1... | collective-permute-start | bytes 786440 | tf_op jit(solution)/shard_map/ppermute | solution.py:123
  198.1 9.1 %collective-permute-start.2 = (f32[1,8,64,128]{3,2,1,0:T(8,128)S(1)}, f32[1,8,64,128]{3,2,1,0:T(8,128)S(1)}, u32[]{:S(2)}, u32[]{:S(2)}) collective-permute-start(f32[1,8,64,128]{3,2,1,0:T(8,128)S(1)} %collective-permute-done.1), channel_id=1, source_target_pairs={{0,1},{1,2},{2,3},{3,4},{4,5},{5,6},{6,7},{7,0},{8,9},{9,10},{10,1... | collective-permute-start | bytes 786440 | tf_op jit(solution)/shard_map/ppermute | solution.py:123
  207.8 9.1 %collective-permute-start.3 = (f32[1,8,64,128]{3,2,1,0:T(8,128)S(1)}, f32[1,8,64,128]{3,2,1,0:T(8,128)S(1)}, u32[]{:S(2)}, u32[]{:S(2)}) collective-permute-start(f32[1,8,64,128]{3,2,1,0:T(8,128)S(1)} %collective-permute-done.2), channel_id=1, source_target_pairs={{0,1},{1,2},{2,3},{3,4},{4,5},{5,6},{6,7},{7,0},{8,9},{9,10},{10,1... | collective-permute-start | bytes 786440 | tf_op jit(solution)/shard_map/ppermute | solution.py:123
  217.6 9.1 %collective-permute-start.4 = (f32[1,8,64,128]{3,2,1,0:T(8,128)S(1)}, f32[1,8,64,128]{3,2,1,0:T(8,128)S(1)}, u32[]{:S(2)}, u32[]{:S(2)}) collective-permute-start(f32[1,8,64,128]{3,2,1,0:T(8,128)S(1)} %collective-permute-done.3), channel_id=1, source_target_pairs={{0,1},{1,2},{2,3},{3,4},{4,5},{5,6},{6,7},{7,0},{8,9},{9,10},{10,1... | collective-permute-start | bytes 786440 | tf_op jit(solution)/shard_map/ppermute | solution.py:123
  227.4 10.0 %collective-permute-start.5 = (f32[1,8,64,128]{3,2,1,0:T(8,128)S(1)}, f32[1,8,64,128]{3,2,1,0:T(8,128)}, u32[]{:S(2)}, u32[]{:S(2)}) collective-permute-start(f32[1,8,64,128]{3,2,1,0:T(8,128)S(1)} %collective-permute-done.4), channel_id=1, source_target_pairs={{0,1},{1,2},{2,3},{3,4},{4,5},{5,6},{6,7},{7,0},{8,9},{9,10},{10,1... | collective-permute-start | bytes 786440 | tf_op jit(solution)/shard_map/ppermute | solution.py:123
  237.4 9.4 %collective-permute-start.6 = (f32[1,8,64,128]{3,2,1,0:T(8,128)}, f32[1,8,64,128]{3,2,1,0:T(8,128)}, u32[]{:S(2)}, u32[]{:S(2)}) collective-permute-start(f32[1,8,64,128]{3,2,1,0:T(8,128)} %collective-permute-done.5), channel_id=1, source_target_pairs={{0,1},{1,2},{2,3},{3,4},{4,5},{5,6},{6,7},{7,0},{8,9},{9,10},{10,1... | collective-permute-start | bytes 786440 | tf_op jit(solution)/shard_map/ppermute | solution.py:123
  239.7 11.1 %copy-start.14 = (f32[1,8,64,128]{3,2,1,0:T(8,128)S(1)}, f32[1,8,64,128]{3,2,1,0:T(8,128)}, u32[]{:S(2)}) copy-start(f32[1,8,64,128]{3,2,1,0:T(8,128)} %copy-done.13) | copy-start | bytes 786436
  239.7 11.1 %copy-start.12 = (f32[1,8,64,128]{3,2,1,0:T(8,128)S(1)}, f32[1,8,64,128]{3,2,1,0:T(8,128)}, u32[]{:S(2)}) copy-start(f32[1,8,64,128]{3,2,1,0:T(8,128)} %copy-done.11) | copy-start | bytes 786436
  239.7 11.2 %copy-start.10 = (f32[1,8,64,128]{3,2,1,0:T(8,128)S(1)}, f32[1,8,64,128]{3,2,1,0:T(8,128)}, u32[]{:S(2)}) copy-start(f32[1,8,64,128]{3,2,1,0:T(8,128)} %copy-done.9) | copy-start | bytes 786436
  248.7 4.2 %copy-start.18 = (f32[1,8,64,128]{3,2,1,0:T(8,128)S(1)}, f32[1,8,64,128]{3,2,1,0:T(8,128)}, u32[]{:S(2)}) copy-start(f32[1,8,64,128]{3,2,1,0:T(8,128)} %copy-done.17) | copy-start | bytes 786436
  259.6 4.5 %copy-start.1 = (f32[4,256,128]{2,1,0:T(8,128)}, f32[4,256,128]{2,1,0:T(8,128)S(1)}, u32[]{:S(2)}) copy-start(f32[4,256,128]{2,1,0:T(8,128)S(1)} %get-tuple-element.897) | copy-start | bytes 1572868 | tf_op jit(solution)/shard_map/transpose(jvp())/while
  259.6 4.5 %copy-start.27 = (f32[8]{0:T(128)}, f32[8]{0:T(128)S(1)}, u32[]{:S(2)}) copy-start(f32[8]{0:T(128)S(1)} %get-tuple-element.777) | copy-start | bytes 100 | tf_op jit(solution)/shard_map/transpose(jvp())/while
  266.8 4.4 %copy-start.25 = (f32[256,8]{0,1:T(8,128)}, f32[256,8]{0,1:T(8,128)S(1)}, u32[]{:S(2)}) copy-start(f32[256,8]{0,1:T(8,128)S(1)} %get-tuple-element.788) | copy-start | bytes 24580 | tf_op jit(solution)/shard_map/transpose(jvp())/while
  278.4 3.3 copy-start.7
  278.4 6.0 %copy-start.23 = (f32[8]{0:T(128)S(1)}, f32[8]{0:T(128)}, u32[]{:S(2)}) copy-start(f32[8]{0:T(128)} %copy-done.22) | copy-start | bytes 100 | tf_op jit(solution)/shard_map/transpose(jvp())/while
  278.4 5.9 %copy-start.24 = (f32[256,8]{0,1:T(8,128)S(1)}, f32[256,8]{0,1:T(8,128)}, u32[]{:S(2)}) copy-start(f32[256,8]{0,1:T(8,128)} %get-tuple-element.798) | copy-start | bytes 24580 | tf_op jit(solution)/shard_map/transpose(jvp())/while
  278.4 5.9 %copy-start.28 = (f32[8]{0:T(128)S(1)}, f32[8]{0:T(128)}, u32[]{:S(2)}) copy-start(f32[8]{0:T(128)} %copy-done.27) | copy-start | bytes 100 | tf_op jit(solution)/shard_map/transpose(jvp())/while
  278.4 6.6 %copy-start.2 = (f32[4,256,128]{2,1,0:T(8,128)S(1)}, f32[4,256,128]{2,1,0:T(8,128)}, u32[]{:S(2)}) copy-start(f32[4,256,128]{2,1,0:T(8,128)} %copy-done.1) | copy-start | bytes 1572868 | tf_op jit(solution)/shard_map/transpose(jvp())/while
  285.0 4.5 %copy-start.1 = (f32[4,256,128]{2,1,0:T(8,128)}, f32[4,256,128]{2,1,0:T(8,128)S(1)}, u32[]{:S(2)}) copy-start(f32[4,256,128]{2,1,0:T(8,128)S(1)} %get-tuple-element.897) | copy-start | bytes 1572868 | tf_op jit(solution)/shard_map/transpose(jvp())/while
  285.0 4.5 %copy-start.27 = (f32[8]{0:T(128)}, f32[8]{0:T(128)S(1)}, u32[]{:S(2)}) copy-start(f32[8]{0:T(128)S(1)} %get-tuple-element.777) | copy-start | bytes 100 | tf_op jit(solution)/shard_map/transpose(jvp())/while
  292.3 4.4 %copy-start.25 = (f32[256,8]{0,1:T(8,128)}, f32[256,8]{0,1:T(8,128)S(1)}, u32[]{:S(2)}) copy-start(f32[256,8]{0,1:T(8,128)S(1)} %get-tuple-element.788) | copy-start | bytes 24580 | tf_op jit(solution)/shard_map/transpose(jvp())/while
  303.8 3.3 copy-start.7
  303.8 6.0 %copy-start.23 = (f32[8]{0:T(128)S(1)}, f32[8]{0:T(128)}, u32[]{:S(2)}) copy-start(f32[8]{0:T(128)} %copy-done.22) | copy-start | bytes 100 | tf_op jit(solution)/shard_map/transpose(jvp())/while
  303.8 5.9 %copy-start.24 = (f32[256,8]{0,1:T(8,128)S(1)}, f32[256,8]{0,1:T(8,128)}, u32[]{:S(2)}) copy-start(f32[256,8]{0,1:T(8,128)} %get-tuple-element.798) | copy-start | bytes 24580 | tf_op jit(solution)/shard_map/transpose(jvp())/while
  303.9 5.9 %copy-start.28 = (f32[8]{0:T(128)S(1)}, f32[8]{0:T(128)}, u32[]{:S(2)}) copy-start(f32[8]{0:T(128)} %copy-done.27) | copy-start | bytes 100 | tf_op jit(solution)/shard_map/transpose(jvp())/while
  303.9 6.6 %copy-start.2 = (f32[4,256,128]{2,1,0:T(8,128)S(1)}, f32[4,256,128]{2,1,0:T(8,128)}, u32[]{:S(2)}) copy-start(f32[4,256,128]{2,1,0:T(8,128)} %copy-done.1) | copy-start | bytes 1572868 | tf_op jit(solution)/shard_map/transpose(jvp())/while
  310.5 4.5 %copy-start.1 = (f32[4,256,128]{2,1,0:T(8,128)}, f32[4,256,128]{2,1,0:T(8,128)S(1)}, u32[]{:S(2)}) copy-start(f32[4,256,128]{2,1,0:T(8,128)S(1)} %get-tuple-element.897) | copy-start | bytes 1572868 | tf_op jit(solution)/shard_map/transpose(jvp())/while
  310.5 4.5 %copy-start.27 = (f32[8]{0:T(128)}, f32[8]{0:T(128)S(1)}, u32[]{:S(2)}) copy-start(f32[8]{0:T(128)S(1)} %get-tuple-element.777) | copy-start | bytes 100 | tf_op jit(solution)/shard_map/transpose(jvp())/while
  317.7 4.4 %copy-start.25 = (f32[256,8]{0,1:T(8,128)}, f32[256,8]{0,1:T(8,128)S(1)}, u32[]{:S(2)}) copy-start(f32[256,8]{0,1:T(8,128)S(1)} %get-tuple-element.788) | copy-start | bytes 24580 | tf_op jit(solution)/shard_map/transpose(jvp())/while
  329.3 3.3 copy-start.7
  329.3 6.0 %copy-start.23 = (f32[8]{0:T(128)S(1)}, f32[8]{0:T(128)}, u32[]{:S(2)}) copy-start(f32[8]{0:T(128)} %copy-done.22) | copy-start | bytes 100 | tf_op jit(solution)/shard_map/transpose(jvp())/while
  329.3 5.9 %copy-start.24 = (f32[256,8]{0,1:T(8,128)S(1)}, f32[256,8]{0,1:T(8,128)}, u32[]{:S(2)}) copy-start(f32[256,8]{0,1:T(8,128)} %get-tuple-element.798) | copy-start | bytes 24580 | tf_op jit(solution)/shard_map/transpose(jvp())/while
  329.3 5.9 %copy-start.28 = (f32[8]{0:T(128)S(1)}, f32[8]{0:T(128)}, u32[]{:S(2)}) copy-start(f32[8]{0:T(128)} %copy-done.27) | copy-start | bytes 100 | tf_op jit(solution)/shard_map/transpose(jvp())/while
  329.3 6.6 %copy-start.2 = (f32[4,256,128]{2,1,0:T(8,128)S(1)}, f32[4,256,128]{2,1,0:T(8,128)}, u32[]{:S(2)}) copy-start(f32[4,256,128]{2,1,0:T(8,128)} %copy-done.1) | copy-start | bytes 1572868 | tf_op jit(solution)/shard_map/transpose(jvp())/while
  335.9 4.5 %copy-start.1 = (f32[4,256,128]{2,1,0:T(8,128)}, f32[4,256,128]{2,1,0:T(8,128)S(1)}, u32[]{:S(2)}) copy-start(f32[4,256,128]{2,1,0:T(8,128)S(1)} %get-tuple-element.897) | copy-start | bytes 1572868 | tf_op jit(solution)/shard_map/transpose(jvp())/while
  335.9 4.5 %copy-start.27 = (f32[8]{0:T(128)}, f32[8]{0:T(128)S(1)}, u32[]{:S(2)}) copy-start(f32[8]{0:T(128)S(1)} %get-tuple-element.777) | copy-start | bytes 100 | tf_op jit(solution)/shard_map/transpose(jvp())/while
  343.2 4.4 %copy-start.25 = (f32[256,8]{0,1:T(8,128)}, f32[256,8]{0,1:T(8,128)S(1)}, u32[]{:S(2)}) copy-start(f32[256,8]{0,1:T(8,128)S(1)} %get-tuple-element.788) | copy-start | bytes 24580 | tf_op jit(solution)/shard_map/transpose(jvp())/while
  354.7 3.3 copy-start.7
  354.7 5.9 %copy-start.23 = (f32[8]{0:T(128)S(1)}, f32[8]{0:T(128)}, u32[]{:S(2)}) copy-start(f32[8]{0:T(128)} %copy-done.22) | copy-start | bytes 100 | tf_op jit(solution)/shard_map/transpose(jvp())/while
  354.7 5.9 %copy-start.24 = (f32[256,8]{0,1:T(8,128)S(1)}, f32[256,8]{0,1:T(8,128)}, u32[]{:S(2)}) copy-start(f32[256,8]{0,1:T(8,128)} %get-tuple-element.798) | copy-start | bytes 24580 | tf_op jit(solution)/shard_map/transpose(jvp())/while
  354.7 5.9 %copy-start.28 = (f32[8]{0:T(128)S(1)}, f32[8]{0:T(128)}, u32[]{:S(2)}) copy-start(f32[8]{0:T(128)} %copy-done.27) | copy-start | bytes 100 | tf_op jit(solution)/shard_map/transpose(jvp())/while
  354.7 6.6 %copy-start.2 = (f32[4,256,128]{2,1,0:T(8,128)S(1)}, f32[4,256,128]{2,1,0:T(8,128)}, u32[]{:S(2)}) copy-start(f32[4,256,128]{2,1,0:T(8,128)} %copy-done.1) | copy-start | bytes 1572868 | tf_op jit(solution)/shard_map/transpose(jvp())/while
  (24 other events, 45.7 us)
Sparse Core Ops, SparseCore 0:
  16.0 51.8 all-gather.3
  365.2 22.0 reduce-scatter.1
